TPU v7x, 32 devices: a whole 2x2x4 slice. The times are simulated.
32 devices in a mesh: grp: 2 (over x), tile: 8 (over z, y), wave: 2 (over core).
Axes of the slice: x: 2, y: 2, z: 4, core: 2. Of those that a mesh axis runs over, the one named last changes fastest.
Arguments:
- residual: float32 [16, 8, 2, 8, 128], P(('grp', 'tile'), 'wave'), parts along dimension 0, may hold values from -210 to 210
- kernel: bfloat16 [16, 8, 9, 2, 128, 128], P(('grp', 'tile'), 'wave'), parts along dimension 0, may hold values from -0.125 to 0.125
- offsets: float32 [16, 8, 2, 128], P(('grp', 'tile'), 'wave'), parts along dimension 0, may hold values from 0 to 1
- neighbor: int32 [16, 8, 9], P(('grp', 'tile'), 'wave'), parts along dimension 0, may hold values from 0 to 8, each once within a row
- frequency: int32 [16], P('grp'), parts along dimension 0, may hold values from 0 to 7, each once
- lattice_x: int32 [128], replicated, may hold values from 0 to 127, each once
- lattice_y: int32 [128], replicated, may hold values from 0 to 127, each once
- spectral_weight: float32 [8, 128, 128], replicated, may hold values from 0.1 to 3
Outputs:
- image_two: float32 [16, 8, 2, 8, 128], P(('grp', 'tile'), 'wave'), parts along dimension 0
- arnoldi: float32 [8, 8], P('grp'), parts along dimension 0
There are 2 independent parts, one for each index of `grp`. A program takes and returns all parts, laid end to end along the dimension named above; an argument that names none is the same for every part. Nothing has to cross between parts.
Inputs may be any that keep to these rules, and one draw needn't show every extreme that they name: `neighbor`: each row names each of the nine neighbour slots once. `frequency`: each index appears once. `lattice_x`: each index appears once. `lattice_y`: each index appears once.
All inputs are finite; a program needn't handle non-finite values.
Results may differ from a plain program's by a relative error of at most 0.013.
Values may be sent and summed in bfloat16 or wider, within the bound.
A program may use at most 64 MiB of HBM per device.

v0:
```python
import math

import jax
import jax.numpy as jnp
from jax import lax
from jax.sharding import PartitionSpec as P

two_pi = 2.0 * math.pi
eps_norm = 1e-06


def padded_2(array, sides, width):
    for axis, dim in sides:
        size, length = (lax.axis_size(axis), array.shape[dim])
        up = [(i, (i + 1) % size) for i in range(size)]
        down = [(j, i) for i, j in up]
        last = lax.slice_in_dim(array, length - width, length, axis=dim)
        initial = lax.slice_in_dim(array, 0, width, axis=dim)
        before = lax.ppermute(last, axis, up)
        after = lax.ppermute(initial, axis, down)
        array = jnp.concatenate([before, array, after], axis=dim)
    return array


def phase_table(position, harmonic):
    phase_angle = two_pi * (position[:, None] * harmonic[None, :])
    return (jnp.cos(phase_angle).astype(jnp.bfloat16), jnp.sin(phase_angle).astype(jnp.bfloat16))


def project_rows(cosine_cols, sine_cols, twisted):
    row_count = cosine_cols.shape[1]
    stacked = jnp.concatenate([cosine_cols, sine_cols], 1)
    gram_matrix = lax.dot_general(
        stacked, twisted, (((0,), (0,)), ((), ())), preferred_element_type=jnp.float32
    )
    gram_matrix = gram_matrix.reshape(2, row_count, 2, -1)
    coef_real = gram_matrix[0, :, 0] + gram_matrix[1, :, 1]
    coef_imag = gram_matrix[0, :, 1] - gram_matrix[1, :, 0]
    return jnp.stack([coef_real, coef_imag], 1)


def expand_rows(cosine_cols, sine_cols, scaled):
    row_count = scaled.shape[0]
    upper_rows = scaled.reshape(row_count, -1)
    lower_rows = jnp.stack([-scaled[:, 1], scaled[:, 0]], 1).reshape(row_count, -1)
    matrix = jnp.concatenate([upper_rows, lower_rows], 0)
    stacked = jnp.concatenate([cosine_cols, sine_cols], 1)
    return jnp.dot(stacked, matrix, preferred_element_type=jnp.float32)


def twist_density(panel_density, cosine_y, sine_y):
    density_real = panel_density[:, 0, :, None].astype(jnp.float32)
    density_imag = panel_density[:, 1, :, None].astype(jnp.float32)
    wave_cos = cosine_y.astype(jnp.float32)[:, None, :]
    wave_sin = sine_y.astype(jnp.float32)[:, None, :]
    part_real = wave_cos * density_real + wave_sin * density_imag
    part_imag = wave_cos * density_imag - wave_sin * density_real
    return (
        jnp.stack([part_real, part_imag], 1)
        .reshape(panel_density.shape[0], -1)
        .astype(jnp.bfloat16)
    )


def finish(summed, cosine_y, sine_y, vectors):
    shaped = summed.reshape(summed.shape[0], 2, vectors, -1)
    wave_cos = cosine_y.astype(jnp.float32)[:, None, :]
    wave_sin = sine_y.astype(jnp.float32)[:, None, :]
    far_real = jnp.sum(shaped[:, 0] * wave_cos - shaped[:, 1] * wave_sin, -1)
    far_imag = jnp.sum(shaped[:, 0] * wave_sin + shaped[:, 1] * wave_cos, -1)
    return jnp.stack([far_real, far_imag], 1)


def combine_near(product, vectors):
    first_half = product[:, 0]
    second = product[:, 1]
    near_real = first_half[:, :vectors] - second[:, vectors:]
    near_imag = second[:, :vectors] + first_half[:, vectors:]
    return jnp.stack([near_real, near_imag], 1)


def panel_sum(values):
    return jnp.sum(values, axis=(0, 1, 3))


def per_device(
    residual, kernel, offsets, neighbor, frequency, lattice_x, lattice_y, spectral_weight
):
    strips = residual.shape[0]
    tiles_y = residual.shape[1]
    vectors = residual.shape[3]
    panels_t = residual.shape[4]
    modes_x = spectral_weight.shape[1]
    modes_y = spectral_weight.shape[2]
    count_x = lax.axis_size("tile") * strips
    count_y = lax.axis_size("wave") * tiles_y
    devices = lax.axis_size("tile") * lax.axis_size("wave")
    panels = count_x * count_y * panels_t
    local_rows = strips * tiles_y * panels_t
    column = (lax.axis_index("tile") * strips + jnp.arange(strips)).astype(jnp.float32)
    row_index = (lax.axis_index("wave") * tiles_y + jnp.arange(tiles_y)).astype(jnp.float32)
    position_x = ((column[:, None, None] + offsets[:, :, 0, :]) / count_x).reshape(-1)
    position_y = ((row_index[None, :, None] + offsets[:, :, 1, :]) / count_y).reshape(-1)
    harmonic_x = (lattice_x - modes_x // 2).astype(jnp.float32)
    harmonic_y = (lattice_y - modes_y // 2).astype(jnp.float32)
    cosine_x, sine_x = phase_table(position_x, harmonic_x)
    cosine_y, sine_y = phase_table(position_y, harmonic_y)
    weight_rows = jnp.take(spectral_weight, frequency, axis=0)
    factor = weight_rows * (1.0 / math.sqrt(modes_x * modes_y * panels))
    factor_wide = jnp.transpose(factor, (1, 0, 2)).reshape(modes_x, vectors * modes_y)[:, None, :]

    def near_field(density):
        padded = padded_2(density, (("tile", 0), ("wave", 1)), 1)
        candidates = []
        for slot_index in range(9):
            shift_x = slot_index // 3 - 1
            shift_y = slot_index % 3 - 1
            candidates.append(
                padded[1 + shift_x : 1 + shift_x + strips, 1 + shift_y : 1 + shift_y + tiles_y]
            )
        stacked = jnp.stack(candidates, 2).reshape(strips * tiles_y, 9, -1)
        picked = jnp.take_along_axis(stacked, neighbor.reshape(strips * tiles_y, 9, 1), axis=1)
        picked = picked.reshape(strips * tiles_y, 9, 2 * vectors, panels_t)
        blocks = kernel.reshape(strips * tiles_y, 9, 2, panels_t, panels_t)
        product = jnp.einsum("tjmp,tjcpq->tcmq", picked, blocks, preferred_element_type=jnp.float32)
        return combine_near(product, vectors).reshape(strips, tiles_y, 2, vectors, panels_t)

    def far_field(density):
        panel_density = jnp.transpose(density, (0, 1, 4, 2, 3)).reshape(local_rows, 2, vectors)
        twisted = twist_density(panel_density, cosine_y, sine_y)
        partial_coeffs = project_rows(cosine_x, sine_x, twisted)
        share_rows = modes_x // devices
        shares = lax.psum_scatter(partial_coeffs, ("tile", "wave"), scatter_dimension=0, tiled=True)
        owner_index = lax.axis_index("tile") * lax.axis_size("wave") + lax.axis_index("wave")
        owner_factor = lax.dynamic_slice_in_dim(
            factor_wide, owner_index * share_rows, share_rows, 0
        )
        owner_scaled = (shares * owner_factor).astype(jnp.bfloat16)
        scaled = lax.all_gather(owner_scaled, ("tile", "wave"), axis=0, tiled=True)
        summed = expand_rows(cosine_x, sine_x, scaled)
        far_panel = finish(summed, cosine_y, sine_y, vectors)
        return far_panel.reshape(strips, tiles_y, panels_t, 2, vectors).transpose(0, 1, 3, 4, 2)

    def apply_operator(density):
        return 0.5 * density.astype(jnp.float32) + near_field(density) + far_field(density)

    local_sq = panel_sum(
        residual[:, :, 0] * residual[:, :, 0] + residual[:, :, 1] * residual[:, :, 1]
    )
    squares = lax.psum(local_sq, ("tile", "wave"))
    basis_scale = jnp.sqrt(squares / panels + eps_norm)
    basis_one = (residual / basis_scale[None, None, None, :, None]).astype(jnp.bfloat16)
    image_one = apply_operator(basis_one)
    basis_real = basis_one[:, :, 0].astype(jnp.float32)
    basis_imag = basis_one[:, :, 1].astype(jnp.float32)
    image_real = image_one[:, :, 0]
    image_imag = image_one[:, :, 1]
    inner_real, inner_imag = lax.psum(
        (
            panel_sum(basis_real * image_real + basis_imag * image_imag),
            panel_sum(basis_real * image_imag - basis_imag * image_real),
        ),
        ("tile", "wave"),
    )
    coef_real = inner_real / panels
    coef_imag = inner_imag / panels
    wide_real = coef_real[None, None, :, None]
    wide_imag = coef_imag[None, None, :, None]
    update_real = image_real - (wide_real * basis_real - wide_imag * basis_imag)
    update_imag = image_imag - (wide_real * basis_imag + wide_imag * basis_real)
    update_sq = lax.psum(
        panel_sum(update_real * update_real + update_imag * update_imag), ("tile", "wave")
    )
    update_scale = jnp.sqrt(update_sq / panels + eps_norm)
    next_basis = (
        jnp.stack([update_real, update_imag], 2) / update_scale[None, None, None, :, None]
    ).astype(jnp.bfloat16)
    image_two = apply_operator(next_basis)
    arnoldi = jnp.stack([basis_scale, coef_real, coef_imag, update_scale])
    return (image_two, arnoldi)


def solution(mesh):
    return jax.shard_map(
        per_device,
        mesh=mesh,
        in_specs=(
            P(("grp", "tile"), "wave", None, None, None),
            P(("grp", "tile"), "wave", None, None, None, None),
            P(("grp", "tile"), "wave", None, None),
            P(("grp", "tile"), "wave", None),
            P("grp"),
            P(),
            P(),
            P(),
        ),
        out_specs=(P(("grp", "tile"), "wave", None, None, None), P("grp", None)),
        check_vma=False,
    )
```

profile of v0, /device:TPU:0, one launch (start us, length us, event | category | flops | bytes accessed | tf_op | source)
XLA Modules:
  0.0 307.0 jit_solution(9363511399105179548)
XLA Ops:
  8.2 34.9 %psum.28 = f32[8]{0:T(128)S(1)} all-reduce(f32[8]{0:T(128)S(1)} %add_reduce_fusion.2), channel_id=1, replica_groups=mesh['grp'=2,'tile'=8,'wave'=2] {'tile','wave'}, use_global_device_ids=true, to_apply=%region_1.2 | all-reduce | flops 8 | bytes 64 | tf_op jit(solution)/shard_map/psum | solution.py:150
  43.7 1.4 fusion.22
  45.2 4.7 %collective-permute-start.1 = (bf16[1,4,2,8,128]{4,3,1,2,0:T(8,128)(2,1)}, bf16[1,4,2,8,128]{4,3,1,2,0:T(8,128)(2,1)}, u32[]{:S(2)}, u32[]{:S(2)}) collective-permute-start(bf16[1,4,2,8,128]{4,3,1,2,0:T(8,128)(2,1)} %fusion.22), channel_id=1, source_target_pairs={{2,0},{4,2},{6,4},{8,6},{10,8},{12,10},{14,12},{0,14},{3,1},{5,3},... | collective-permute-start | bytes 49160 | tf_op jit(solution)/shard_map/ppermute | solution.py:20
  54.7 1.1 cosine_convert_fusion.1
  56.9 1.1 pad_maximum_fusion.2
  58.7 1.6 gather_fusion
  61.7 1.2 copy.121
  63.0 1.3 pad_maximum_fusion.31
  67.8 1.2 copy.122
  73.7 1.5 gather_fusion.1
  76.5 36.3 %reduce-scatter.3.cloned.1.call-done = f32[8,2,1024]{2,0,1:T(8,128)} async-done(((f32[128,2,1024]{2,0,1:T(8,128)}), f32[8,2,1024]{2,0,1:T(8,128)}) %reduce-scatter.3.cloned.1.call-update) | async-done | bytes 65552 | tf_op jit(solution)/shard_map/reduce_scatter | solution.py:133
  113.7 20.8 %all_gather.6 = bf16[128,2,1024]{2,0,1:T(8,128)(2,1)S(1)} all-gather(bf16[8,2,1024]{2,0,1:T(8,128)(2,1)S(1)} %multiply_convert_fusion.1), channel_id=1, replica_groups=mesh['grp'=2,'tile'=8,'wave'=2] {'tile','wave'}, dimensions={0}, use_global_device_ids=true | all-gather | bytes 557056 | tf_op jit(solution)/shard_map/all_gather | solution.py:139
  136.3 1.1 pad_maximum_fusion.4
  138.4 2.0 convolution_bitcast_fusion.1
  141.4 1.2 subtract_reduce_fusion.1
  145.2 29.8 %all-reduce = (f32[8]{0:T(128)S(1)}, f32[8]{0:T(128)S(1)}) all-reduce(f32[8]{0:T(128)S(1)} %get-tuple-element.16, f32[8]{0:T(128)S(1)} %get-tuple-element.15), channel_id=1, replica_groups=mesh['grp'=2,'tile'=8,'wave'=2] {'tile','wave'}, use_global_device_ids=true, to_apply=%region_8.10 | all-reduce | flops 16 | bytes 128 | tf_op jit(solution)/shard_map/psum | solution.py:158
  176.7 29.5 %psum.31 = f32[8]{0:T(128)S(1)} all-reduce(f32[8]{0:T(128)S(1)} %fusion.40), channel_id=1, replica_groups=mesh['grp'=2,'tile'=8,'wave'=2] {'tile','wave'}, use_global_device_ids=true, to_apply=%region_10.12 | all-reduce | flops 8 | bytes 64 | tf_op jit(solution)/shard_map/psum | solution.py:171
  206.4 4.7 %collective-permute-start.5 = (bf16[1,4,2,8,128]{4,3,1,2,0:T(8,128)(2,1)S(1)}, bf16[1,4,2,8,128]{4,3,1,2,0:T(8,128)(2,1)S(1)}, u32[]{:S(2)}, u32[]{:S(2)}) collective-permute-start(bf16[1,4,2,8,128]{4,3,1,2,0:T(8,128)(2,1)S(1)} %fusion.20), channel_id=1, source_target_pairs={{2,0},{4,2},{6,4},{8,6},{10,8},{12,10},{14,12},{0,14},{3,1},{5,3},... | collective-permute-start | bytes 49160 | tf_op jit(solution)/shard_map/ppermute | solution.py:20
  213.7 1.1 pad_maximum_fusion.3
  217.2 1.5 gather_fusion.2
  219.4 50.2 %reduce-scatter.5.cloned.1.call-done = f32[8,2,1024]{2,0,1:T(8,128)} async-done(((f32[128,2,1024]{2,0,1:T(8,128)}), f32[8,2,1024]{2,0,1:T(8,128)}) %reduce-scatter.5.cloned.1.call-update) | async-done | bytes 65552 | tf_op jit(solution)/shard_map/reduce_scatter | solution.py:133
  270.5 20.8 %all_gather.7 = bf16[128,2,1024]{2,0,1:T(8,128)(2,1)S(1)} all-gather(bf16[8,2,1024]{2,0,1:T(8,128)(2,1)S(1)} %multiply_convert_fusion), channel_id=1, replica_groups=mesh['grp'=2,'tile'=8,'wave'=2] {'tile','wave'}, dimensions={0}, use_global_device_ids=true | all-gather | bytes 557056 | tf_op jit(solution)/shard_map/all_gather | solution.py:139
  295.1 2.0 convolution_bitcast_fusion
  298.1 1.2 subtract_reduce_fusion
  (197 shorter events, 39.9 us)
Async XLA Ops:
  7.2 68.3 %copy-start = (bf16[1,4,9,2,128,128]{5,4,3,2,1,0:T(8,128)(2,1)S(1)}, bf16[1,4,9,2,128,128]{5,4,3,2,1,0:T(8,128)(2,1)}, u32[]{:S(2)}) copy-start(bf16[1,4,9,2,128,128]{5,4,3,2,1,0:T(8,128)(2,1)} %param.11) | copy-start | bytes 7077892
  7.2 105.6 %reduce-scatter.3.cloned.1.call-start = ((), (), s32[]{:S(2)}) async-start(), calls=%async_computation.2 | async-start | bytes 1114112 | tf_op jit(solution)/shard_map/reduce_scatter | solution.py:133
  43.7 7.0 %copy-start.19 = (f32[8]{0:T(128)}, f32[8]{0:T(128)S(1)}, u32[]{:S(2)}) copy-start(f32[8]{0:T(128)S(1)} %get-tuple-element.68) | copy-start | bytes 100
  45.2 17.8 %collective-permute-start = (bf16[1,4,2,8,128]{4,3,1,2,0:T(8,128)(2,1)}, bf16[1,4,2,8,128]{4,3,1,2,0:T(8,128)(2,1)}, u32[]{:S(2)}, u32[]{:S(2)}) collective-permute-start(bf16[1,4,2,8,128]{4,3,1,2,0:T(8,128)(2,1)} %fusion.22), channel_id=1, source_target_pairs={{0,2},{2,4},{4,6},{6,8},{8,10},{10,12},{12,14},{14,0},{1,3},{3,5},... | collective-permute-start | bytes 49160 | tf_op jit(solution)/shard_map/ppermute | solution.py:19
  45.2 17.8 %collective-permute-start.1 = (bf16[1,4,2,8,128]{4,3,1,2,0:T(8,128)(2,1)}, bf16[1,4,2,8,128]{4,3,1,2,0:T(8,128)(2,1)}, u32[]{:S(2)}, u32[]{:S(2)}) collective-permute-start(bf16[1,4,2,8,128]{4,3,1,2,0:T(8,128)(2,1)} %fusion.22), channel_id=1, source_target_pairs={{2,0},{4,2},{6,4},{8,6},{10,8},{12,10},{14,12},{0,14},{3,1},{5,3},... | collective-permute-start | bytes 49160 | tf_op jit(solution)/shard_map/ppermute | solution.py:20
  53.9 12.3 %copy-start.1 = (f32[512,128]{0,1:T(8,128)}, f32[512,128]{0,1:T(8,128)S(1)}, u32[]{:S(2)}) copy-start(f32[512,128]{0,1:T(8,128)S(1)} %get-tuple-element.64) | copy-start | bytes 786436
  58.0 211.7 %reduce-scatter.5.cloned.1.call-start = ((), (), s32[]{:S(2)}) async-start(), calls=%async_computation.3 | async-start | bytes 1114112 | tf_op jit(solution)/shard_map/reduce_scatter | solution.py:133
  64.3 7.5 %collective-permute-start.2 = (bf16[3,1,2,8,128]{4,3,1,2,0:T(8,128)(2,1)}, bf16[3,1,2,8,128]{4,3,1,2,0:T(8,128)(2,1)}, u32[]{:S(2)}, u32[]{:S(2)}) collective-permute-start(bf16[3,1,2,8,128]{4,3,1,2,0:T(8,128)(2,1)} %get-tuple-element.56), channel_id=1, source_target_pairs={{0,1},{1,0},{2,3},{3,2},{4,5},{5,4},{6,7},{7,6},{8,9},{9,8},{10,11... | collective-permute-start | bytes 36872 | tf_op jit(solution)/shard_map/ppermute | solution.py:19
  67.7 7.5 %copy-start.21 = (pred[4,9]{1,0:T(4,128)(4,1)S(1)}, pred[4,9]{1,0:T(4,128)(4,1)}, u32[]{:S(2)}) copy-start(pred[4,9]{1,0:T(4,128)(4,1)} %and_bitcast_fusion) | copy-start | bytes 112
  69.0 43.9 %copy-start.16 = (f32[8,1,1024]{2,0,1:T(8,128)}, f32[8,1,1024]{2,0,1:T(8,128)S(1)}, u32[]{:S(2)}) copy-start(f32[8,1,1024]{2,0,1:T(8,128)S(1)} %copy.122) | copy-start | bytes 98308
  70.5 2.1 collective-permute-start.3
  134.4 4.0 %copy-start.10 = (bf16[512,128]{0,1:T(8,128)(2,1)S(1)}, bf16[512,128]{0,1:T(8,128)(2,1)}, u32[]{:S(2)}) copy-start(bf16[512,128]{0,1:T(8,128)(2,1)} %copy-done.9) | copy-start | bytes 393220
  141.4 2.0 copy-start.20
  141.4 69.8 %copy-start.2 = (f32[512,128]{0,1:T(8,128)S(1)}, f32[512,128]{0,1:T(8,128)}, u32[]{:S(2)}) copy-start(f32[512,128]{0,1:T(8,128)} %copy-done.1) | copy-start | bytes 786436
  176.7 38.0 %copy-start.12 = (f32[1,4,1,8,128]{4,3,1,2,0:T(8,128)}, f32[1,4,1,8,128]{4,3,1,2,0:T(8,128)S(1)}, u32[]{:S(2)}) copy-start(f32[1,4,1,8,128]{4,3,1,2,0:T(8,128)S(1)} %get-tuple-element.51) | copy-start | bytes 49156
  176.7 38.0 %copy-start.14 = (f32[1,4,1,8,128]{4,3,1,2,0:T(8,128)}, f32[1,4,1,8,128]{4,3,1,2,0:T(8,128)S(1)}, u32[]{:S(2)}) copy-start(f32[1,4,1,8,128]{4,3,1,2,0:T(8,128)S(1)} %get-tuple-element.52) | copy-start | bytes 49156
  206.4 8.4 %collective-permute-start.4 = (bf16[1,4,2,8,128]{4,3,1,2,0:T(8,128)(2,1)S(1)}, bf16[1,4,2,8,128]{4,3,1,2,0:T(8,128)(2,1)S(1)}, u32[]{:S(2)}, u32[]{:S(2)}) collective-permute-start(bf16[1,4,2,8,128]{4,3,1,2,0:T(8,128)(2,1)S(1)} %fusion.20), channel_id=1, source_target_pairs={{0,2},{2,4},{4,6},{6,8},{8,10},{10,12},{12,14},{14,0},{1,3},{3,5},... | collective-permute-start | bytes 49160 | tf_op jit(solution)/shard_map/ppermute | solution.py:19
  206.4 8.4 %collective-permute-start.5 = (bf16[1,4,2,8,128]{4,3,1,2,0:T(8,128)(2,1)S(1)}, bf16[1,4,2,8,128]{4,3,1,2,0:T(8,128)(2,1)S(1)}, u32[]{:S(2)}, u32[]{:S(2)}) collective-permute-start(bf16[1,4,2,8,128]{4,3,1,2,0:T(8,128)(2,1)S(1)} %fusion.20), channel_id=1, source_target_pairs={{2,0},{4,2},{6,4},{8,6},{10,8},{12,10},{14,12},{0,14},{3,1},{5,3},... | collective-permute-start | bytes 49160 | tf_op jit(solution)/shard_map/ppermute | solution.py:20
  214.8 4.0 %copy-start.22 = (pred[4,9]{1,0:T(4,128)(4,1)S(1)}, pred[4,9]{1,0:T(4,128)(4,1)}, u32[]{:S(2)}) copy-start(pred[4,9]{1,0:T(4,128)(4,1)} %and_bitcast_fusion) | copy-start | bytes 112
  214.8 1.2 collective-permute-start.7
  215.5 1.3 collective-permute-start.6
  218.7 51.0 %copy-start.17 = (f32[8,1,1024]{2,0,1:T(8,128)S(1)}, f32[8,1,1024]{2,0,1:T(8,128)}, u32[]{:S(2)}) copy-start(f32[8,1,1024]{2,0,1:T(8,128)} %copy-done.16) | copy-start | bytes 98308
  291.3 3.8 %copy-start.11 = (bf16[512,128]{0,1:T(8,128)(2,1)S(1)}, bf16[512,128]{0,1:T(8,128)(2,1)}, u32[]{:S(2)}) copy-start(bf16[512,128]{0,1:T(8,128)(2,1)} %copy-done.9) | copy-start | bytes 393220
  298.0 1.4 copy-start.15
  (11 other events, 11.5 us)
Sparse Core Ops, SparseCore 0:
  58.1 54.6 reduce-scatter.2
  214.9 54.7 reduce-scatter.4
where the time goes:
time: 308 us; the launch traced here: 307 us
  blocking collectives  136 us (44%)
  waiting for transfers between devices  87.3 us (28%)
  other arithmetic  30 us (10%)
  local copies, waits for them, and re-layouts  22.2 us (7%)
  between operations  14.9 us (5%)
  starting transfers between devices  10.7 us (3%)
  matrix products  6.26 us (2%)
    reduce_scatter x2, waiting for transfers between devices, far_field(): lax.psum_scatter(partial_coeffs, ('tile', 'wave'), scatter_dimension=0, t...  86.5 us
    all_gather x2, blocking collectives, far_field(): scaled = lax.all_gather(owner_scaled, ('tile', 'wave'), axis=0, tiled=True)  41.5 us
    psum x1, blocking collectives, per_device(): squares = lax.psum(local_sq, ('tile', 'wave'))  34.9 us
    psum x1, blocking collectives, per_device(): lax.psum((panel_sum(basis_real * image_real + basis_imag * image_imag), p...  29.8 us
    psum x1, blocking collectives, per_device(): lax.psum(panel_sum(update_real * update_real + update_imag * update_imag)...  29.5 us
    ppermute x4, starting transfers between devices, padded_2(): after = lax.ppermute(initial, axis, down)  10.1 us
  transfers between devices with their start and end apart: 10, of which 3 were waited for; matrix products, arithmetic and copies ran while one was open for 10% of the time, Pallas kernels for 0%

commit v1 on v0

v1 whole, which is shorter than its diff:
```python
import functools
import math

import jax
import jax.numpy as jnp
from jax import lax
from jax.experimental import pallas as pl
from jax.experimental.pallas import tpu as pltpu
from jax.sharding import PartitionSpec as P

eps_norm = 1e-06
f32 = jnp.float32
bf16 = jnp.bfloat16
MESH = pl.DeviceIdType.MESH

cos_poly = (
    0.9999999890754361,
    -19.739204500992756,
    64.93911749755512,
    -85.45013994334624,
    60.167632824407875,
    -25.967602439336652,
    6.528658637171564,
)
sin_poly = (
    6.283185302518495,
    -41.3417004059728,
    81.60513140266713,
    -76.70301552901445,
    42.02592777896992,
    -14.89984800704947,
    3.2381376825656845,
)


def horner(coefs, z):
    total = coefs[-1] * z + coefs[-2]
    for c in coefs[-3::-1]:
        total = total * z + c
    return total


def cos_sin(turns):
    r = turns - jnp.round(turns)
    z = r * r
    return horner(cos_poly, z), r * horner(sin_poly, z)


def rows_dot(a, b):
    return lax.dot_general(a, b, (((1,), (1,)), ((), ())), preferred_element_type=f32)


def body(
    size_t,
    size_w,
    tiles,
    vectors,
    modes_x,
    modes_y,
    residual,
    blocks,
    offsets,
    neighbor,
    frequency,
    lattice_x,
    lattice_y,
    weight,
    image_out,
    arnoldi_out,
    send_a,
    recv_a,
    send_f1,
    recv_f1,
    send_r,
    recv_r,
    send_b,
    recv_b,
    send_f2,
    recv_f2,
    halo_1,
    halo_2,
    table_x,
    cos_y,
    sin_y,
    harm_x,
    harm_y,
    fact,
    image,
    basis,
    kernel_vmem,
    kernel_sem,
    send_sem,
    recv_sem,
    halo_send,
    halo_recv,
):
    devices = size_t * size_w
    shares = devices // vectors
    rows_b = modes_y // shares
    slots = 2 * tiles
    lanes = 128
    panels = devices * tiles * lanes
    count_x = size_t
    count_y = size_w * tiles
    t = lax.axis_index("tile")
    w = lax.axis_index("wave")
    me = t * size_w + w
    my_vector = me // shares
    my_share = lax.rem(me, shares)

    barrier = pltpu.get_barrier_semaphore()

    def place(index):
        return {"tile": index // size_w, "wave": lax.rem(index, size_w)}

    def greet(k, carry):
        other = lax.rem(me + k, devices)
        pl.semaphore_signal(barrier, inc=1, device_id=place(other), device_id_type=MESH)
        return carry

    lax.fori_loop(1, devices, greet, 0)
    load = pltpu.make_async_copy(blocks, kernel_vmem, kernel_sem)
    load.start()

    def exchange_start(phase, source, target):
        def step(k, carry):
            other = lax.rem(me + k, devices)
            pltpu.make_async_remote_copy(
                src_ref=source(other),
                dst_ref=target.at[me],
                send_sem=send_sem.at[phase],
                recv_sem=recv_sem.at[phase],
                device_id=place(other),
                device_id_type=MESH,
            ).start()
            return carry

        lax.fori_loop(1, devices, step, 0)

    def exchange_wait(phase, target):
        part = target.at[pl.ds(0, devices - 1)]
        pltpu.make_async_copy(part, part, recv_sem.at[phase]).wait()

    def sent_wait(phase, target):
        part = target.at[pl.ds(0, devices - 1)]
        pltpu.make_async_copy(part, part, send_sem.at[phase]).wait()

    up = lax.rem(t + 1, size_t)
    down = lax.rem(t + size_t - 1, size_t)
    other_w = lax.rem(w + 1, size_w)

    def halo_copies(phase, halo):
        copies = []
        targets = ((up, w, 0), (up, other_w, 0), (t, other_w, 1), (down, w, 2), (down, other_w, 2))
        for number, (to_t, to_w, row) in enumerate(targets):
            copies.append(
                pltpu.make_async_remote_copy(
                    src_ref=halo.at[1, pl.ds(w * tiles, tiles)],
                    dst_ref=halo.at[row, pl.ds(w * tiles, tiles)],
                    send_sem=halo_send.at[phase, number],
                    recv_sem=halo_recv.at[phase, number],
                    device_id={"tile": to_t, "wave": to_w},
                    device_id_type=MESH,
                )
            )
        return copies

    def stage(values, halo, slab):
        for h in range(tiles):
            rounded = [values[h][c].astype(bf16) for c in range(2)]
            for c in range(2):
                wide = rounded[c].astype(f32)
                basis[h, c] = wide
                slab[:, c * tiles + h, :] = wide
            halo[1, w * tiles + h] = jnp.concatenate(rounded, 0)

    first = [[residual[h, c] for c in range(2)] for h in range(tiles)]
    stage(first, halo_1, send_a)
    offset_rows = offsets[...].reshape(slots, lanes)
    for v in range(vectors):
        send_a[v, slots : 2 * slots, :] = offset_rows
    pl.semaphore_wait(barrier, devices - 1)
    copies_1 = halo_copies(0, halo_1)
    exchange_start(0, lambda other: send_a.at[other // shares], recv_a)
    for copy in copies_1:
        copy.start()
    recv_a[me] = send_a[my_vector]

    square = jnp.zeros((vectors, lanes), f32)
    for h in range(tiles):
        for c in range(2):
            square += residual[h, c] * residual[h, c]

    wave_x = (lattice_x[...] - modes_x // 2).astype(f32)
    harm_x[...] = jnp.broadcast_to(wave_x, (lanes, modes_x)).T
    wave_y = (lattice_y[...] - modes_y // 2).astype(f32)
    harm_y[...] = jnp.broadcast_to(wave_y, (lanes, modes_y)).T
    my_weight = weight[frequency[my_vector]]
    fact[...] = (my_weight * (1.0 / math.sqrt(modes_x * modes_y * panels))).T
    share_rows = pl.ds(pl.multiple_of(my_share * rows_b, rows_b), rows_b)
    hx = harm_x[...]
    hy = harm_y[share_rows, :]
    factor = fact[share_rows, :]

    exchange_wait(0, recv_a)

    def project(with_tables, recv):
        def step(d, total):
            twisted = []
            for h in range(tiles):
                cols = slice(h * lanes, (h + 1) * lanes)
                if with_tables:
                    g = (d // size_w).astype(f32)
                    column = (lax.rem(d, size_w) * tiles + h).astype(f32)
                    off_x = recv[d, slots + 2 * h : slots + 2 * h + 1, :]
                    off_y = recv[d, slots + 2 * h + 1 : slots + 2 * h + 2, :]
                    px = (g + off_x) / count_x
                    py = (column + off_y) / count_y
                    cos_a, sin_a = cos_sin(px * hx)
                    table_x[d, 0:modes_x, cols] = cos_a.astype(bf16)
                    table_x[d, modes_x : 2 * modes_x, cols] = sin_a.astype(bf16)
                    cos_b, sin_b = cos_sin(py * hy)
                    cy = cos_b.astype(bf16).astype(f32)
                    sy = sin_b.astype(bf16).astype(f32)
                    cos_y[d, :, cols] = cy
                    sin_y[d, :, cols] = sy
                else:
                    cy = cos_y[d, :, cols]
                    sy = sin_y[d, :, cols]
                q_r = recv[d, h : h + 1, :]
                q_i = recv[d, tiles + h : tiles + h + 1, :]
                twisted.append(
                    jnp.concatenate([cy * q_r + sy * q_i, cy * q_i - sy * q_r], 0).astype(bf16)
                )
            return total + rows_dot(jnp.concatenate(twisted, 1), table_x[d])

        return lax.fori_loop(0, devices, step, jnp.zeros((2 * rows_b, 2 * modes_x), f32))

    def far_partial(total, slab):
        top = total[:rows_b]
        low = total[rows_b:]
        real = top[:, :modes_x] + low[:, modes_x:]
        imag = low[:, :modes_x] - top[:, modes_x:]
        real = (real * factor).astype(bf16)
        imag = (imag * factor).astype(bf16)
        matrix = jnp.concatenate(
            [jnp.concatenate([real, -imag], 1), jnp.concatenate([imag, real], 1)], 0
        )

        def step(d, carry):
            summed = jnp.dot(matrix, table_x[d], preferred_element_type=f32)
            s_r = summed[:rows_b]
            s_i = summed[rows_b:]
            cy = cos_y[d]
            sy = sin_y[d]
            far_r = jnp.sum(s_r * cy - s_i * sy, 0, keepdims=True)
            far_i = jnp.sum(s_r * sy + s_i * cy, 0, keepdims=True)
            for h in range(tiles):
                cols = slice(h * lanes, (h + 1) * lanes)
                slab[d, h : h + 1, :] = far_r[:, cols]
                slab[d, tiles + h : tiles + h + 1, :] = far_i[:, cols]
            return carry

        lax.fori_loop(0, devices, step, 0)

    def near_and_half(halo):
        for h in range(tiles):
            picked = []
            for j in range(9):
                slot = neighbor[h * 9 + j]
                row = slot // 3
                column = lax.rem(w * tiles + h + lax.rem(slot, 3) - 1 + count_y, count_y)
                picked.append(halo[row, column])
            left = jnp.concatenate(picked, 1)
            right = jnp.concatenate(
                [
                    jnp.concatenate([kernel_vmem[h, j, c] for j in range(9)], 0)
                    for c in range(2)
                ],
                1,
            )
            product = jnp.dot(left, right, preferred_element_type=f32)
            image[h, 0] = (
                0.5 * basis[h, 0] + product[:vectors, :lanes] - product[vectors:, lanes:]
            )
            image[h, 1] = (
                0.5 * basis[h, 1] + product[:vectors, lanes:] + product[vectors:, :lanes]
            )

    def far_of(recv, row):
        grouped = recv[:, row, :].reshape(vectors, shares, lanes)
        return jnp.sum(grouped, 1)

    def far_own(slab, recv):
        recv[me, 0:slots, :] = slab[me, 0:slots, :]

    far_partial(project(True, recv_a), send_f1)
    exchange_start(1, lambda other: send_f1.at[other], recv_f1)
    far_own(send_f1, recv_f1)
    load.wait()
    for copy in copies_1:
        copy.wait_recv()
    near_and_half(halo_1)
    exchange_wait(1, recv_f1)

    inner_r = jnp.zeros((vectors, lanes), f32)
    inner_i = jnp.zeros((vectors, lanes), f32)
    for h in range(tiles):
        w_r = image[h, 0] + far_of(recv_f1, h)
        w_i = image[h, 1] + far_of(recv_f1, tiles + h)
        image[h, 0] = w_r
        image[h, 1] = w_i
        b_r = basis[h, 0]
        b_i = basis[h, 1]
        inner_r += b_r * w_r + b_i * w_i
        inner_i += b_r * w_i - b_i * w_r
    lane = lax.broadcasted_iota(jnp.int32, (vectors, lanes), 1)
    sums = [jnp.sum(x, 1, keepdims=True) for x in (square, inner_r, inner_i)]
    send_r[...] = jnp.where(lane == 0, sums[0], jnp.where(lane == 1, sums[1], sums[2]))
    exchange_start(2, lambda other: send_r, recv_r)
    recv_r[me] = send_r[...]
    exchange_wait(2, recv_r)
    sums = jnp.sum(recv_r[...], 0)
    scale = jnp.sqrt(sums[:, 0:1] / panels + eps_norm)
    inverse = 1.0 / scale
    inverse_2 = inverse * inverse
    coef_r = sums[:, 1:2] / panels * inverse_2
    coef_i = sums[:, 2:3] / panels * inverse_2

    square = jnp.zeros((vectors, lanes), f32)
    second = []
    for h in range(tiles):
        b_r = basis[h, 0]
        b_i = basis[h, 1]
        u_r = (image[h, 0] - (coef_r * b_r - coef_i * b_i)) * inverse
        u_i = (image[h, 1] - (coef_r * b_i + coef_i * b_r)) * inverse
        square += u_r * u_r + u_i * u_i
        second.append((u_r, u_i))
    stage(second, halo_2, send_b)
    copies_2 = halo_copies(1, halo_2)
    exchange_start(3, lambda other: send_b.at[other // shares], recv_b)
    for copy in copies_2:
        copy.start()
    recv_b[me] = send_b[my_vector]

    def put_square(d, carry):
        send_f2[d, slots : slots + vectors, :] = square
        return carry

    lax.fori_loop(0, devices, put_square, 0)
    exchange_wait(3, recv_b)
    far_partial(project(False, recv_b), send_f2)
    exchange_start(4, lambda other: send_f2.at[other], recv_f2)
    recv_f2[me] = send_f2[me]
    for copy in copies_2:
        copy.wait_recv()
    near_and_half(halo_2)
    exchange_wait(4, recv_f2)
    update_sq = jnp.sum(recv_f2[:, slots : slots + vectors, :], 0)
    update_sq = jnp.sum(update_sq, 1, keepdims=True)
    update_scale = jnp.sqrt(update_sq / panels + eps_norm)
    inverse = 1.0 / update_scale
    for h in range(tiles):
        for c in range(2):
            image_out[h, c] = (image[h, c] + far_of(recv_f2, c * tiles + h)) * inverse
    row = lax.broadcasted_iota(jnp.int32, (vectors, lanes), 0)
    for number, value in enumerate((scale, coef_r, coef_i, update_scale)):
        line = jnp.sum(jnp.where(row == lane, value, 0.0), 0, keepdims=True)
        arnoldi_out[number : number + 1, :] = line[:, :vectors]

    for copy in copies_1 + copies_2:
        copy.wait_send()
    for phase, target in enumerate((recv_a, recv_f1, recv_r, recv_b, recv_f2)):
        sent_wait(phase, target)


def per_device(
    size_t,
    size_w,
    residual,
    kernel,
    offsets,
    neighbor,
    frequency,
    lattice_x,
    lattice_y,
    spectral_weight,
):
    strips, tiles, _, vectors, lanes = residual.shape
    modes_x, modes_y = spectral_weight.shape[1:]
    devices = size_t * size_w
    assert strips == 1 and lanes == 128 and size_w == 2 and size_t > 2
    assert devices % vectors == 0
    rows_b = modes_y // (devices // vectors)
    slots = 2 * tiles
    vmem = pl.BlockSpec(memory_space=pltpu.VMEM)
    smem = pl.BlockSpec(memory_space=pltpu.SMEM)
    halo = pltpu.VMEM((3, size_w * tiles, 2 * vectors, lanes), bf16)
    image, arnoldi = pl.pallas_call(
        functools.partial(body, size_t, size_w, tiles, vectors, modes_x, modes_y),
        out_shape=(
            jax.ShapeDtypeStruct((tiles, 2, vectors, lanes), f32),
            jax.ShapeDtypeStruct((4, vectors), f32),
        ),
        in_specs=[
            vmem,
            pl.BlockSpec(memory_space=pl.ANY),
            vmem,
            smem,
            smem,
            vmem,
            vmem,
            vmem,
        ],
        out_specs=(vmem, vmem),
        scratch_shapes=[
            pltpu.VMEM((vectors, 2 * slots, lanes), f32),
            pltpu.VMEM((devices, 2 * slots, lanes), f32),
            pltpu.VMEM((devices, slots, lanes), f32),
            pltpu.VMEM((devices, slots, lanes), f32),
            pltpu.VMEM((vectors, lanes), f32),
            pltpu.VMEM((devices, vectors, lanes), f32),
            pltpu.VMEM((vectors, slots, lanes), f32),
            pltpu.VMEM((devices, slots, lanes), f32),
            pltpu.VMEM((devices, slots + vectors, lanes), f32),
            pltpu.VMEM((devices, slots + vectors, lanes), f32),
            halo,
            halo,
            pltpu.VMEM((devices, 2 * modes_x, tiles * lanes), bf16),
            pltpu.VMEM((devices, rows_b, tiles * lanes), f32),
            pltpu.VMEM((devices, rows_b, tiles * lanes), f32),
            pltpu.VMEM((modes_x, lanes), f32),
            pltpu.VMEM((modes_y, lanes), f32),
            pltpu.VMEM((modes_y, modes_x), f32),
            pltpu.VMEM((tiles, 2, vectors, lanes), f32),
            pltpu.VMEM((tiles, 2, vectors, lanes), f32),
            pltpu.VMEM((tiles, 9, 2, lanes, lanes), bf16),
            pltpu.SemaphoreType.DMA,
            pltpu.SemaphoreType.DMA((5,)),
            pltpu.SemaphoreType.DMA((5,)),
            pltpu.SemaphoreType.DMA((2, 5)),
            pltpu.SemaphoreType.DMA((2, 5)),
        ],
        compiler_params=pltpu.CompilerParams(
            collective_id=0, has_side_effects=True, vmem_limit_bytes=56 * 1024 * 1024
        ),
        name="arnoldi_pair",
    )(
        residual[0],
        kernel[0],
        offsets[0],
        neighbor.reshape(-1),
        frequency,
        lattice_x[None],
        lattice_y[None],
        spectral_weight,
    )
    return image[None], arnoldi


def solution(mesh):
    return jax.shard_map(
        functools.partial(per_device, mesh.shape["tile"], mesh.shape["wave"]),
        mesh=mesh,
        in_specs=(
            P(("grp", "tile"), "wave", None, None, None),
            P(("grp", "tile"), "wave", None, None, None, None),
            P(("grp", "tile"), "wave", None, None),
            P(("grp", "tile"), "wave", None),
            P("grp"),
            P(),
            P(),
            P(),
        ),
        out_specs=(P(("grp", "tile"), "wave", None, None, None), P("grp", None)),
        check_vma=False,
    )
```

time: 308 us -> 56.3 us (0.18)
  blocking collectives: 136 us -> 0 us
  waiting for transfers between devices: 87.3 us -> 0 us
  Pallas kernels: 0 us -> 51.5 us
  other arithmetic: 30 us -> 0 us
  local copies, waits for them, and re-layouts: 22.2 us -> 3.89 us
  between operations: 14.9 us -> 0.64 us
  starting transfers between devices: 10.7 us -> 0 us
  matrix products: 6.26 us -> 0 us
    psum x3 -> x0, blocking collectives: 94.2 us -> none  [the longest x1 34.9 us: per_device(): squares = lax.psum(local_sq, ('tile', 'wave'))]
    reduce_scatter x2 -> x0, waiting for transfers between devices: 86.5 us -> none  [far_field(): lax.psum_scatter(partial_coeffs, ('tile', 'wave'), scatter_dimension=0, t...]
    pallas_call x0 -> x1, Pallas kernels: none -> 51.5 us  [per_device(): pl.pallas_call(functools.partial(body, size_t, size_w, tiles, vectors, mo...]
    all_gather x2 -> x0, blocking collectives: 41.5 us -> none  [far_field(): scaled = lax.all_gather(owner_scaled, ('tile', 'wave'), axis=0, tiled=True)]
    ppermute x8 -> x0, starting transfers between devices: 10.6 us -> none  [the longest x4 10.1 us: padded_2(): after = lax.ppermute(initial, axis, down)]
    another operation x15 -> x0, other arithmetic: 7.55 us -> none  [the longest x2 2.13 us: project_rows(): return jnp.stack([coef_real, coef_imag], 1)]
    convert_element_type x11 -> x0, other arithmetic: 6.68 us -> none  [the longest x2 1.7 us: far_field(): owner_scaled = (shares * owner_factor).astype(jnp.bfloat16)]
    dot_general x6 -> x0, matrix products: 6.26 us -> none  [the longest x2 3.93 us: expand_rows(): return jnp.dot(stacked, matrix, preferred_element_type=jnp.float32)]
  transfers between devices with their start and end apart: 10 -> 0, of which waited for: 3 -> 0; matrix products, arithmetic and copies ran while one was open for 10% -> 0% of each run, Pallas kernels for 0% -> 0%
where the time goes in v1:
time: 56.3 us; the launch traced here: 56 us
  Pallas kernels  51.5 us (91%)
  local copies, waits for them, and re-layouts  3.89 us (7%)
  between operations  0.64 us (1%)
    pallas_call x1, Pallas kernels, per_device(): pl.pallas_call(functools.partial(body, size_t, size_w, tiles, vectors, mo...  51.5 us
    unnamed x2, local copies, waits for them, and re-layouts  2.62 us
    reshape x1, local copies, waits for them, and re-layouts, per_device(): neighbor.reshape(-1)  1.27 us

profile of v1, /device:TPU:0, one launch (start us, length us, event | category | flops | bytes accessed | tf_op | source)
XLA Modules:
  0.0 56.0 jit_solution(4871381409302213029)
XLA Ops:
  0.6 1.3 %reshape.7.neighbor = s32[36]{0:T(128)} reshape(s32[1,4,9]{2,1,0:T(4,128)} %param.11) | data formatting | bytes 288 | tf_op jit(solution)/shard_map/reshape | solution.py:452
  1.9 51.5 %arnoldi_pair.1 = (f32[4,2,8,128]{3,2,1,0:T(8,128)}, f32[4,8]{1,0:T(4,128)}) custom-call(f32[4,2,8,128]{3,2,1,0:T(8,128)} %bitcast.7, bf16[4,9,2,128,128]{4,3,2,1,0:T(8,128)(2,1)} %bitcast.6, f32[4,2,128]{2,1,0:T(2,128)} %bitcast.9, s32[36]{0:T(128)} %reshape.7.neighbor, s32[8]{0:T(128)} %frequency.1, s32[1,128]{1,0:T(1,128)} %bitcast.10, ...), custom_call_target="tpu_custom_call" | custom-call | tf_op jit(solution)/shard_map/arnoldi_pair/pallas_call | solution.py:399
  53.4 1.4 %copy.12 = f32[1,4,2,8,128]{4,3,2,1,0:T(8,128)} copy(f32[1,4,2,8,128]{4,3,2,1,0:T(8,128)} %bitcast.8) | data formatting | bytes 65536
  54.8 1.2 %copy.13 = f32[4,8]{1,0:T(4,128)} copy(f32[4,8]{1,0:T(4,128)} %get-tuple-element.9) | data formatting | bytes 256

commit v2 on v1

--- a/solution.py
+++ b/solution.py
@@ -9,6 +9,8 @@
 from jax.sharding import PartitionSpec as P
 
 eps_norm = 1e-06
+unroll_project = 8
+unroll_expand = 5
 f32 = jnp.float32
 bf16 = jnp.bfloat16
 MESH = pl.DeviceIdType.MESH
@@ -122,17 +124,20 @@
     load = pltpu.make_async_copy(blocks, kernel_vmem, kernel_sem)
     load.start()
 
+    def copy_to(phase, other, source, target):
+        return pltpu.make_async_remote_copy(
+            src_ref=source,
+            dst_ref=target.at[me],
+            send_sem=send_sem.at[phase],
+            recv_sem=recv_sem.at[phase],
+            device_id=place(other),
+            device_id_type=MESH,
+        )
+
     def exchange_start(phase, source, target):
         def step(k, carry):
             other = lax.rem(me + k, devices)
-            pltpu.make_async_remote_copy(
-                src_ref=source(other),
-                dst_ref=target.at[me],
-                send_sem=send_sem.at[phase],
-                recv_sem=recv_sem.at[phase],
-                device_id=place(other),
-                device_id_type=MESH,
-            ).start()
+            copy_to(phase, other, source(other), target).start()
             return carry
 
         lax.fori_loop(1, devices, step, 0)
@@ -234,9 +239,10 @@
                 )
             return total + rows_dot(jnp.concatenate(twisted, 1), table_x[d])
 
-        return lax.fori_loop(0, devices, step, jnp.zeros((2 * rows_b, 2 * modes_x), f32))
-
-    def far_partial(total, slab):
+        zero = jnp.zeros((2 * rows_b, 2 * modes_x), f32)
+        return lax.fori_loop(0, devices, step, zero, unroll=unroll_project)
+
+    def far_partial(total, slab, phase, target):
         top = total[:rows_b]
         low = total[rows_b:]
         real = top[:, :modes_x] + low[:, modes_x:]
@@ -247,7 +253,7 @@
             [jnp.concatenate([real, -imag], 1), jnp.concatenate([imag, real], 1)], 0
         )
 
-        def step(d, carry):
+        def expand(d):
             summed = jnp.dot(matrix, table_x[d], preferred_element_type=f32)
             s_r = summed[:rows_b]
             s_i = summed[rows_b:]
@@ -259,15 +265,21 @@
                 cols = slice(h * lanes, (h + 1) * lanes)
                 slab[d, h : h + 1, :] = far_r[:, cols]
                 slab[d, tiles + h : tiles + h + 1, :] = far_i[:, cols]
+
+        def step(k, carry):
+            d = lax.rem(me + k, devices)
+            expand(d)
+            copy_to(phase, d, slab.at[d], target).start()
             return carry
 
-        lax.fori_loop(0, devices, step, 0)
+        lax.fori_loop(1, devices, step, 0, unroll=unroll_expand)
+        expand(me)
 
     def near_and_half(halo):
         for h in range(tiles):
             picked = []
             for j in range(9):
-                slot = neighbor[h * 9 + j]
+                slot = neighbor[0, h, j]
                 row = slot // 3
                 column = lax.rem(w * tiles + h + lax.rem(slot, 3) - 1 + count_y, count_y)
                 picked.append(halo[row, column])
@@ -294,8 +306,7 @@
     def far_own(slab, recv):
         recv[me, 0:slots, :] = slab[me, 0:slots, :]
 
-    far_partial(project(True, recv_a), send_f1)
-    exchange_start(1, lambda other: send_f1.at[other], recv_f1)
+    far_partial(project(True, recv_a), send_f1, 1, recv_f1)
     far_own(send_f1, recv_f1)
     load.wait()
     for copy in copies_1:
@@ -349,8 +360,7 @@
 
     lax.fori_loop(0, devices, put_square, 0)
     exchange_wait(3, recv_b)
-    far_partial(project(False, recv_b), send_f2)
-    exchange_start(4, lambda other: send_f2.at[other], recv_f2)
+    far_partial(project(False, recv_b), send_f2, 4, recv_f2)
     recv_f2[me] = send_f2[me]
     for copy in copies_2:
         copy.wait_recv()
@@ -372,6 +382,11 @@
         copy.wait_send()
     for phase, target in enumerate((recv_a, recv_f1, recv_r, recv_b, recv_f2)):
         sent_wait(phase, target)
+
+
+def hand_over(image, arnoldi, image_out, arnoldi_out):
+    image_out[...] = image[...]
+    arnoldi_out[...] = arnoldi[...]
 
 
 def per_device(
@@ -449,12 +464,22 @@
         residual[0],
         kernel[0],
         offsets[0],
-        neighbor.reshape(-1),
+        neighbor,
         frequency,
         lattice_x[None],
         lattice_y[None],
         spectral_weight,
     )
+    image, arnoldi = pl.pallas_call(
+        hand_over,
+        out_shape=(
+            jax.ShapeDtypeStruct(image.shape, f32),
+            jax.ShapeDtypeStruct(arnoldi.shape, f32),
+        ),
+        in_specs=[vmem, vmem],
+        out_specs=(vmem, vmem),
+        name="hand_over",
+    )(image, arnoldi)
     return image[None], arnoldi
 
 

time: 56.3 us -> 45.3 us (0.80)
  Pallas kernels: 51.5 us -> 44.4 us
  local copies, waits for them, and re-layouts: 3.89 us -> 0 us
    pallas_call x1, Pallas kernels: 51.5 us -> 43 us  [per_device(): pl.pallas_call(functools.partial(body, size_t, size_w, tiles, vectors, mo...]
    unnamed x2 -> x0, local copies, waits for them, and re-layouts: 2.62 us -> none
    pallas_call x0 -> x1, Pallas kernels: none -> 1.38 us  [per_device(): pl.pallas_call(hand_over, out_shape=(jax.ShapeDtypeStruct(image.shape, f3...]
    reshape x1 -> x0, local copies, waits for them, and re-layouts: 1.27 us -> none  [per_device(): neighbor.reshape(-1)]
where the time goes in v2:
time: 45.3 us; the launch traced here: 45.1 us
  Pallas kernels  44.4 us (98%)
  between operations  0.64 us (1%)
    pallas_call x1, Pallas kernels, per_device(): pl.pallas_call(functools.partial(body, size_t, size_w, tiles, vectors, mo...  43 us
    pallas_call x1, Pallas kernels, per_device(): pl.pallas_call(hand_over, out_shape=(jax.ShapeDtypeStruct(image.shape, f3...  1.38 us

profile of v2, /device:TPU:0, one launch (start us, length us, event | category | flops | bytes accessed | tf_op | source)
XLA Modules:
  0.0 45.1 jit_solution(14858591326130542500)
XLA Ops:
  0.6 43.0 %arnoldi_pair.1 = (f32[4,2,8,128]{3,2,1,0:T(8,128)}, f32[4,8]{1,0:T(4,128)}) custom-call(f32[4,2,8,128]{3,2,1,0:T(8,128)} %bitcast.7, bf16[4,9,2,128,128]{4,3,2,1,0:T(8,128)(2,1)} %bitcast.6, f32[4,2,128]{2,1,0:T(2,128)} %bitcast.8, s32[1,4,9]{2,1,0:T(4,128)} %neighbor.1, s32[8]{0:T(128)} %frequency.1, s32[1,128]{1,0:T(1,128)} %bitcast.9, ...), custom_call_target="tpu_custom_call" | custom-call | tf_op jit(solution)/shard_map/arnoldi_pair/pallas_call | solution.py:414
  43.7 1.4 %hand_over.1 = (f32[4,2,8,128]{3,2,1,0:T(8,128)}, f32[4,8]{1,0:T(4,128)}) custom-call(f32[4,2,8,128]{3,2,1,0:T(8,128)} %get-tuple-element.6.image, f32[4,8]{1,0:T(4,128)} %get-tuple-element.7.arnoldi), custom_call_target="tpu_custom_call" | custom-call | tf_op jit(solution)/shard_map/hand_over/pallas_call | solution.py:473

commit v3 on v2

--- a/solution.py
+++ b/solution.py
@@ -84,8 +84,6 @@
     table_x,
     cos_y,
     sin_y,
-    harm_x,
-    harm_y,
     fact,
     image,
     basis,
@@ -196,16 +194,33 @@
         for c in range(2):
             square += residual[h, c] * residual[h, c]
 
-    wave_x = (lattice_x[...] - modes_x // 2).astype(f32)
-    harm_x[...] = jnp.broadcast_to(wave_x, (lanes, modes_x)).T
-    wave_y = (lattice_y[...] - modes_y // 2).astype(f32)
-    harm_y[...] = jnp.broadcast_to(wave_y, (lanes, modes_y)).T
-    my_weight = weight[frequency[my_vector]]
-    fact[...] = (my_weight * (1.0 / math.sqrt(modes_x * modes_y * panels))).T
-    share_rows = pl.ds(pl.multiple_of(my_share * rows_b, rows_b), rows_b)
-    hx = harm_x[...]
-    hy = harm_y[share_rows, :]
-    factor = fact[share_rows, :]
+    my_weight = weight[frequency[my_vector]] * (1.0 / math.sqrt(modes_x * modes_y * panels))
+    row_y = lax.broadcasted_iota(jnp.int32, (modes_y, modes_y), 0)
+    row_x = lax.broadcasted_iota(jnp.int32, (modes_x, modes_x), 0)
+    pick_y = jnp.where(jnp.broadcast_to(lattice_y[...], row_y.shape) == row_y, 1.0, 0.0)
+    pick_x = jnp.where(jnp.broadcast_to(lattice_x[...], row_x.shape) == row_x, 1.0, 0.0)
+    exact = lax.Precision.HIGHEST
+    by_y = jnp.dot(pick_y, my_weight.T, precision=exact, preferred_element_type=f32)
+    fact[...] = jnp.dot(by_y, pick_x.T, precision=exact, preferred_element_type=f32)
+    first_y = my_share * rows_b
+    factor = fact[pl.ds(pl.multiple_of(first_y, rows_b), rows_b), :]
+    groups_y = max(rows_b // 8, 8)
+    low = lax.broadcasted_iota(jnp.int32, (8, lanes), 0).astype(f32)
+    high_x = lax.broadcasted_iota(jnp.int32, (modes_x // 8, lanes), 0) * 8 - modes_x // 2
+    high_y = lax.broadcasted_iota(jnp.int32, (groups_y, lanes), 0) * 8 + (first_y - modes_y // 2)
+    high_x = high_x.astype(f32)
+    high_y = high_y.astype(f32)
+
+    def phases(position, high, rows):
+        cos_l, sin_l = cos_sin(position * low)
+        cos_h, sin_h = cos_sin(position * high)
+        cosines, sines = [], []
+        for m in range(rows // 8):
+            c = jnp.broadcast_to(cos_h[m : m + 1], low.shape)
+            s = jnp.broadcast_to(sin_h[m : m + 1], low.shape)
+            cosines.append(c * cos_l - s * sin_l)
+            sines.append(s * cos_l + c * sin_l)
+        return jnp.concatenate(cosines, 0), jnp.concatenate(sines, 0)
 
     exchange_wait(0, recv_a)
 
@@ -221,10 +236,10 @@
                     off_y = recv[d, slots + 2 * h + 1 : slots + 2 * h + 2, :]
                     px = (g + off_x) / count_x
                     py = (column + off_y) / count_y
-                    cos_a, sin_a = cos_sin(px * hx)
+                    cos_a, sin_a = phases(px, high_x, modes_x)
                     table_x[d, 0:modes_x, cols] = cos_a.astype(bf16)
                     table_x[d, modes_x : 2 * modes_x, cols] = sin_a.astype(bf16)
-                    cos_b, sin_b = cos_sin(py * hy)
+                    cos_b, sin_b = phases(py, high_y, rows_b)
                     cy = cos_b.astype(bf16).astype(f32)
                     sy = sin_b.astype(bf16).astype(f32)
                     cos_y[d, :, cols] = cy
@@ -444,8 +459,6 @@
             pltpu.VMEM((devices, 2 * modes_x, tiles * lanes), bf16),
             pltpu.VMEM((devices, rows_b, tiles * lanes), f32),
             pltpu.VMEM((devices, rows_b, tiles * lanes), f32),
-            pltpu.VMEM((modes_x, lanes), f32),
-            pltpu.VMEM((modes_y, lanes), f32),
             pltpu.VMEM((modes_y, modes_x), f32),
             pltpu.VMEM((tiles, 2, vectors, lanes), f32),
             pltpu.VMEM((tiles, 2, vectors, lanes), f32),

time: 45.3 us -> 42.5 us (0.938)
  Pallas kernels: 44.4 us -> 41.7 us
    pallas_call x1, Pallas kernels: 43 us -> 40.3 us  [per_device(): pl.pallas_call(functools.partial(body, size_t, size_w, tiles, vectors, mo...]
where the time goes in v3:
time: 42.5 us; the launch traced here: 42.3 us
  Pallas kernels  41.7 us (98%)
  between operations  0.64 us (2%)
    pallas_call x1, Pallas kernels, per_device(): pl.pallas_call(functools.partial(body, size_t, size_w, tiles, vectors, mo...  40.3 us
    pallas_call x1, Pallas kernels, per_device(): pl.pallas_call(hand_over, out_shape=(jax.ShapeDtypeStruct(image.shape, f3...  1.38 us

profile of v3, /device:TPU:0, one launch (start us, length us, event | category | flops | bytes accessed | tf_op | source)
XLA Modules:
  0.0 42.3 jit_solution(4962301732718963206)
XLA Ops:
  0.6 40.3 %arnoldi_pair.1 = (f32[4,2,8,128]{3,2,1,0:T(8,128)}, f32[4,8]{1,0:T(4,128)}) custom-call(f32[4,2,8,128]{3,2,1,0:T(8,128)} %bitcast.7, bf16[4,9,2,128,128]{4,3,2,1,0:T(8,128)(2,1)} %bitcast.6, f32[4,2,128]{2,1,0:T(2,128)} %bitcast.8, s32[1,4,9]{2,1,0:T(4,128)} %neighbor.1, s32[8]{0:T(128)} %frequency.1, s32[1,128]{1,0:T(1,128)} %bitcast.9, ...), custom_call_target="tpu_custom_call" | custom-call | tf_op jit(solution)/shard_map/arnoldi_pair/pallas_call | solution.py:429
  40.9 1.4 %hand_over.1 = (f32[4,2,8,128]{3,2,1,0:T(8,128)}, f32[4,8]{1,0:T(4,128)}) custom-call(f32[4,2,8,128]{3,2,1,0:T(8,128)} %get-tuple-element.6.image, f32[4,8]{1,0:T(4,128)} %get-tuple-element.7.arnoldi), custom_call_target="tpu_custom_call" | custom-call | tf_op jit(solution)/shard_map/hand_over/pallas_call | solution.py:486
